TPU v7x, 256 devices: a whole 4x4x8 slice. The times are simulated.
256 devices in a mesh: wide: 32 (over z_lo, y, core), narrow: 8 (over z_hi, x).
Axes of the slice: x: 4, y: 4, z: 8 (z_hi: 2, z_lo: 4; z = z_hi * 4 + z_lo), core: 2. Of those that a mesh axis runs over, the one named last changes fastest.
Arguments:
- gradient: float32 [3072, 3072], P('wide', 'narrow'), may hold values from -6 to 6
- first_moment: float32 [3072, 3072], P('wide', 'narrow'), may hold values from -6 to 6
- second_moment: float32 [3072, 3072], P('wide', 'narrow'), may hold values from 0.25 to 4
- left_basis: float32 [3072, 3072], P('wide', 'narrow'), may hold values from -0.21875 to 0.21875
- right_basis: float32 [3072, 3072], P('wide', 'narrow'), may hold values from -0.109375 to 0.109375
Outputs:
- update: float32 [3072, 3072], P('wide', 'narrow')
- new_first: float32 [3072, 3072], P('wide', 'narrow')
- new_second: float32 [3072, 3072], P('wide', 'narrow')
All inputs are finite; a program needn't handle non-finite values.
Results may differ from a plain program's by a relative error of at most 0.000075.
Values sent between devices are 32-bit elements; how exact they have to be, the bound alone decides.
No kernel may reach another device: no remote copies, remote signals or barrier semaphores. Data moves between devices by JAX's collectives and lax.ppermute only.
A program may use at most 64 MiB of HBM per device.

v0:
```python
import jax
import jax.numpy as jnp
from jax import lax
from jax.sharding import Mesh
from jax.sharding import PartitionSpec as P

STEP = 10
WIDE = ("wide_0", "wide_1", "wide_2")
beta_first = 0.9
beta_second = 0.95
epsilon = 1e-08


def side_by_side(arrays, axis, dim, along):
    ends, at = ([], 0)
    for a in arrays[:-1]:
        at += a.shape[along]
        ends.append(at)
    both = jnp.concatenate(arrays, axis=along)
    return tuple(jnp.split(lax.all_gather(both, axis, axis=dim, tiled=True), ends, axis=along))


def in_blocks(value, dim, peers):
    lengths = value.shape
    tiles = value.reshape(*lengths[:dim], peers, lengths[dim] // peers, *lengths[dim + 1 :])
    return jnp.moveaxis(tiles, dim, 0)


def scatter_pairs(value, chips, core, dim):
    sizes = (lax.axis_size(chips), lax.axis_size(core))
    tiles = in_blocks(value, dim, sizes[0] * sizes[1])
    inside = tiles.shape[1:]
    tiles = tiles.reshape(*sizes, *inside).swapaxes(0, 1).reshape(-1, *inside)
    tiles = lax.psum_scatter(tiles, core, scatter_dimension=0, tiled=True)
    return lax.psum_scatter(tiles, chips, scatter_dimension=0, tiled=True)[0]


def sent_and_summed(value, axis, dim):
    tiles = in_blocks(value, dim, lax.axis_size(axis))
    arrived = lax.all_to_all(tiles, axis, split_axis=0, concat_axis=0, tiled=True)
    return arrived.sum(axis=0)


def product(left, right):
    return jnp.dot(left, right, precision=lax.Precision.HIGHEST, preferred_element_type=jnp.float32)


def contract(left, right, left_dim, right_dim):
    return lax.dot_general(
        left,
        right,
        (((left_dim,), (right_dim,)), ((), ())),
        precision=lax.Precision.HIGHEST,
        preferred_element_type=jnp.float32,
    )


def body(gradient, first_moment, second_moment, left_basis, right_basis):
    grad_rows, left_rows = side_by_side((gradient, left_basis), "narrow", 1, 0)
    right_panel = lax.all_gather(right_basis, WIDE, axis=0, tiled=True)
    rotated_right = product(grad_rows, right_panel)
    columns = left_rows
    rotated = scatter_pairs(
        contract(columns, rotated_right, 0, 0), ("wide_0", "wide_1"), "wide_2", 0
    )
    new_first = beta_first * first_moment + (1.0 - beta_first) * rotated
    new_second = beta_second * second_moment + (1.0 - beta_second) * rotated * rotated
    direction = (
        new_first
        / (1.0 - beta_first**STEP)
        / (jnp.sqrt(new_second / (1.0 - beta_second**STEP)) + epsilon)
    )
    columns = left_rows
    back_left = product(columns, lax.all_gather(direction, WIDE, axis=0, tiled=True))
    terms = contract(back_left, right_panel, 1, 1)
    update = sent_and_summed(terms, "narrow", 1)
    return (update, new_first, new_second)


def solution(mesh):
    torus = Mesh(
        mesh.devices.reshape(4, 4, 2, mesh.shape["narrow"]),
        ("wide_0", "wide_1", "wide_2", "narrow"),
    )
    return jax.shard_map(
        body,
        mesh=torus,
        in_specs=(
            P(WIDE, "narrow"),
            P(WIDE, "narrow"),
            P(WIDE, "narrow"),
            P(WIDE, "narrow"),
            P(WIDE, "narrow"),
        ),
        out_specs=(P(WIDE, "narrow"), P(WIDE, "narrow"), P(WIDE, "narrow")),
        check_vma=False,
    )
```

profile of v0, /device:TPU:32, one launch (start us, length us, event | category | flops | bytes accessed | tf_op | source)
XLA Modules:
  0.0 398.6 jit_solution(4710670992428549391)
XLA Ops:
  7.2 0.0 all-gather.4.cloned.1.call-start
  7.2 1.7 pad_maximum_fusion
  8.9 0.0 all-gather.4.cloned.1.call-update
  9.0 0.0 all-gather.6.cloned.1.call-start
  9.0 0.7 all-gather.6.cloned.1.call-update
  9.7 0.0 reduce-scatter.3.cloned.1.call-start
  9.8 82.1 %all-gather.4.cloned.1.call-done = f32[192,3072]{1,0:T(8,128)} async-done(((f32[192,384]{1,0:T(8,128)}), f32[192,3072]{1,0:T(8,128)}) %all-gather.4.cloned.1.call-update) | async-done | bytes 2359312 | tf_op jit(solution)/shard_map/all_gather | solution.py:20
  91.8 0.0 copy-start
  91.8 62.0 %all-gather.6.cloned.1.call-done = f32[3072,384]{1,0:T(8,128)} async-done(((f32[96,384]{1,0:T(8,128)}), f32[3072,384]{1,0:T(8,128)}) %all-gather.6.cloned.1.call-update) | async-done | bytes 4718608 | tf_op jit(solution)/shard_map/all_gather | solution.py:60
  153.8 5.6 %fusion = f32[96,384]{1,0:T(8,128)S(1)} fusion(f32[3072,384]{1,0:T(8,128)} %all-gather.6.cloned.1.call-done, f32[192,3072]{1,0:T(8,128)} %all-gather.4.cloned.1.call-done), kind=kOutput, calls=%fused_computation.1 | convolution fusion | flops 1358954496 | bytes 6045696 | tf_op jit(solution)/shard_map/dot_general | solution.py:45
  159.4 0.0 copy-done
  159.4 3.9 fusion.4
  163.3 2.5 copy.9
  165.9 0.0 reduce-scatter.3.cloned.1.call-update
  165.9 0.0 copy-start.1
  165.9 0.0 copy-start.2
  165.9 0.0 reduce-scatter.5.cloned.1.call-start
  166.0 17.3 %reduce-scatter.3.cloned.1.call-done = f32[16,96,384]{2,1,0:T(8,128)} async-done(((f32[32,96,384]{2,1,0:T(8,128)}), f32[16,96,384]{2,1,0:T(8,128)}) %reduce-scatter.3.cloned.1.call-update) | async-done | bytes 2359312 | tf_op jit(solution)/shard_map/reduce_scatter | solution.py:34
  183.3 0.0 reduce-scatter.5.cloned.1.call-update
  183.3 0.2 all-gather.8.cloned.1.call-start
  183.5 84.9 %reduce-scatter.5.cloned.1.call-done = f32[1,96,384]{2,1,0:T(8,128)} async-done(((f32[16,96,384]{2,1,0:T(8,128)}), f32[1,96,384]{2,1,0:T(8,128)}) %reduce-scatter.5.cloned.1.call-update) | async-done | bytes 147472 | tf_op jit(solution)/shard_map/reduce_scatter | solution.py:35
  268.4 0.0 copy-done.1
  268.4 0.0 copy-done.2
  268.4 1.7 add_divide_fusion
  270.1 0.0 all-gather.8.cloned.1.call-update
  270.1 67.9 %all-gather.8.cloned.1.call-done = f32[3072,384]{1,0:T(8,128)} async-done(((f32[96,384]{1,0:T(8,128)}), f32[3072,384]{1,0:T(8,128)}) %all-gather.8.cloned.1.call-update) | async-done | bytes 4718608 | tf_op jit(solution)/shard_map/all_gather | solution.py:74
  338.0 5.2 %fusion.2 = f32[96,384]{1,0:T(8,128)S(1)} fusion(f32[3072,384]{1,0:T(8,128)} %all-gather.8.cloned.1.call-done, f32[192,3072]{1,0:T(8,128)S(1)} %copy-done), kind=kOutput, calls=%fused_computation.3 | convolution fusion | flops 1358954496 | bytes 6045696 | tf_op jit(solution)/shard_map/dot_general | solution.py:45
  343.3 6.5 %fusion.10 = f32[96,3072]{1,0:T(8,128)S(1)} fusion(f32[96,384]{1,0:T(8,128)S(1)} %fusion.2, f32[3072,384]{1,0:T(8,128)} %all-gather.6.cloned.1.call-done), kind=kOutput, calls=%fused_computation.13 | convolution fusion | flops 1358954496 | bytes 6045696 | tf_op jit(solution)/shard_map/dot_general | solution.py:49
  349.8 0.1 copy.13
  349.8 41.5 %all_to_all.5 = f32[8,96,384]{2,1,0:T(8,128)S(1)} all-to-all(f32[8,96,384]{2,1,0:T(8,128)S(1)} %bitcast.25), channel_id=1, replica_groups=mesh['wide_0'=4,'wide_1'=4,'wide_2'=2,'narrow'=8] {'narrow'}, dimensions={0} | all-to-all | bytes 2359296 | tf_op jit(solution)/shard_map/all_to_all | solution.py:40
  391.3 0.7 reduce_sum.9
Async XLA Ops:
  7.2 84.6 %all-gather.4.cloned.1.call-start = ((), (), s32[]{:S(2)}) async-start(), calls=%async_computation.3 | async-start | bytes 2654208 | tf_op jit(solution)/shard_map/all_gather | solution.py:20
  9.0 144.8 %all-gather.6.cloned.1.call-start = ((), (), s32[]{:S(2)}) async-start(), calls=%async_computation.4 | async-start | bytes 4866048 | tf_op jit(solution)/shard_map/all_gather | solution.py:60
  9.7 173.6 %reduce-scatter.3.cloned.1.call-start = ((), (), s32[]{:S(2)}) async-start(), calls=%async_computation.5 | async-start | bytes 7077888 | tf_op jit(solution)/shard_map/reduce_scatter | solution.py:34
  91.8 67.6 %copy-start = (f32[192,3072]{1,0:T(8,128)S(1)}, f32[192,3072]{1,0:T(8,128)}, u32[]{:S(2)}) copy-start(f32[192,3072]{1,0:T(8,128)} %all-gather.4.cloned.1.call-done) | copy-start | bytes 7077892
  165.9 102.5 %copy-start.1 = (f32[96,384]{1,0:T(8,128)S(1)}, f32[96,384]{1,0:T(8,128)}, u32[]{:S(2)}) copy-start(f32[96,384]{1,0:T(8,128)} %param.6) | copy-start | bytes 442372
  165.9 102.5 %copy-start.2 = (f32[96,384]{1,0:T(8,128)S(1)}, f32[96,384]{1,0:T(8,128)}, u32[]{:S(2)}) copy-start(f32[96,384]{1,0:T(8,128)} %param.7) | copy-start | bytes 442372
  165.9 102.5 %reduce-scatter.5.cloned.1.call-start = ((), (), s32[]{:S(2)}) async-start(), calls=%async_computation.6 | async-start | bytes 2506752 | tf_op jit(solution)/shard_map/reduce_scatter | solution.py:35
  183.3 154.7 %all-gather.8.cloned.1.call-start = ((), (), s32[]{:S(2)}) async-start(), calls=%async_computation.7 | async-start | bytes 4866048 | tf_op jit(solution)/shard_map/all_gather | solution.py:74
Sparse Core Ops, SparseCore 0:
  10.6 81.1 all-gather.3
  93.7 60.0 all-gather.5
  166.0 17.2 reduce-scatter.2
  185.9 82.5 reduce-scatter.4
  270.8 67.1 all-gather.7
where the time goes:
time: 399 us
  waiting for transfers between devices  315 us (79%)
  blocking collectives  41.5 us (10%)
  matrix products  21.2 us (5%)
  between operations  13.8 us (3%)
  other arithmetic  4.16 us (1%)
    reduce_scatter x1, waiting for transfers between devices, scatter_pairs(): return lax.psum_scatter(tiles, chips, scatter_dimension=0, tiled=True)[0]  84.9 us
    all_gather x1, waiting for transfers between devices, side_by_side(): lax.all_gather(both, axis, axis=dim, tiled=True)  82.1 us
    all_gather x1, waiting for transfers between devices, body(): lax.all_gather(direction, WIDE, axis=0, tiled=True)  67.9 us
    all_gather x1, waiting for transfers between devices, body(): right_panel = lax.all_gather(right_basis, WIDE, axis=0, tiled=True)  62 us
    all_to_all x1, blocking collectives, sent_and_summed(): lax.all_to_all(tiles, axis, split_axis=0, concat_axis=0, tiled=True)  41.5 us
    reduce_scatter x1, waiting for transfers between devices, scatter_pairs(): tiles = lax.psum_scatter(tiles, core, scatter_dimension=0, tiled=True)  17.3 us
    dot_general x2, matrix products, product(): jnp.dot(left, right, precision=lax.Precision.HIGHEST, preferred_element_t...  10.8 us
    dot_general x2, matrix products, contract(): lax.dot_general(left, right, (((left_dim,), (right_dim,)), ((), ())), pre...  10.4 us
  transfers between devices with their start and end apart: 5, of which 5 were waited for; matrix products, arithmetic and copies ran while one was open for 0% of the time, Pallas kernels for 0%

commit v1 on v0

--- a/solution.py
+++ b/solution.py
@@ -9,6 +9,15 @@
 beta_first = 0.9
 beta_second = 0.95
 epsilon = 1e-08
+
+
+def make_the_slot(base_x):
+    return jnp.concatenate(
+        jax.lax.all_to_all(
+            jnp.stack(jax.lax.axis_size(WIDE) * [base_x], axis=0), WIDE, concat_axis=0, split_axis=0
+        ),
+        axis=0,
+    )
 
 
 def side_by_side(arrays, axis, dim, along):
@@ -71,7 +80,7 @@
         / (jnp.sqrt(new_second / (1.0 - beta_second**STEP)) + epsilon)
     )
     columns = left_rows
-    back_left = product(columns, lax.all_gather(direction, WIDE, axis=0, tiled=True))
+    back_left = product(columns, make_the_slot(direction))
     terms = contract(back_left, right_panel, 1, 1)
     update = sent_and_summed(terms, "narrow", 1)
     return (update, new_first, new_second)

time: 399 us -> 444 us (1.11)
  blocking collectives: 41.5 us -> 158 us
  waiting for transfers between devices: 315 us -> 247 us
    all_to_all x0 -> x1, blocking collectives: none -> 116 us  [make_the_slot(): jax.lax.all_to_all(jnp.stack(jax.lax.axis_size(WIDE) * [base_x], axis=0),...]
    all_gather x1 -> x0, waiting for transfers between devices: 67.9 us -> none  [body(): lax.all_gather(direction, WIDE, axis=0, tiled=True)]
  transfers between devices with their start and end apart: 5 -> 4, of which waited for: 5 -> 4; matrix products, arithmetic and copies ran while one was open for 0% -> 0% of each run, Pallas kernels for 0% -> 0%
where the time goes in v1:
time: 444 us
  waiting for transfers between devices  247 us (56%)
  blocking collectives  158 us (36%)
  matrix products  17.1 us (4%)
  between operations  13.9 us (3%)
    all_to_all x1, blocking collectives, make_the_slot(): jax.lax.all_to_all(jnp.stack(jax.lax.axis_size(WIDE) * [base_x], axis=0),...  116 us
    reduce_scatter x1, waiting for transfers between devices, scatter_pairs(): return lax.psum_scatter(tiles, chips, scatter_dimension=0, tiled=True)[0]  85.1 us
    all_gather x1, waiting for transfers between devices, side_by_side(): lax.all_gather(both, axis, axis=dim, tiled=True)  82.1 us
    all_gather x1, waiting for transfers between devices, body(): right_panel = lax.all_gather(right_basis, WIDE, axis=0, tiled=True)  62 us
    all_to_all x1, blocking collectives, sent_and_summed(): lax.all_to_all(tiles, axis, split_axis=0, concat_axis=0, tiled=True)  42.3 us
    reduce_scatter x1, waiting for transfers between devices, scatter_pairs(): tiles = lax.psum_scatter(tiles, core, scatter_dimension=0, tiled=True)  17.3 us
  transfers between devices with their start and end apart: 4, of which 4 were waited for; matrix products, arithmetic and copies ran while one was open for 0% of the time, Pallas kernels for 0%

profile of v1, /device:TPU:32, one launch (start us, length us, event | category | flops | bytes accessed | tf_op | source)
XLA Modules:
  0.0 443.9 jit_solution(5256794154565857879)
XLA Ops:
  7.2 0.0 all-gather.3.cloned.1.call-start
  7.2 1.7 pad_maximum_fusion
  8.9 0.0 all-gather.3.cloned.1.call-update
  8.9 0.0 all-gather.5.cloned.1.call-start
  9.0 0.7 all-gather.5.cloned.1.call-update
  9.7 0.0 reduce-scatter.3.cloned.1.call-start
  9.7 82.1 %all-gather.3.cloned.1.call-done = f32[192,3072]{1,0:T(8,128)} async-done(((f32[192,384]{1,0:T(8,128)}), f32[192,3072]{1,0:T(8,128)}) %all-gather.3.cloned.1.call-update) | async-done | bytes 2359312 | tf_op jit(solution)/shard_map/all_gather | solution.py:29
  91.8 0.0 copy-start
  91.8 62.0 %all-gather.5.cloned.1.call-done = f32[3072,384]{1,0:T(8,128)} async-done(((f32[96,384]{1,0:T(8,128)}), f32[3072,384]{1,0:T(8,128)}) %all-gather.5.cloned.1.call-update) | async-done | bytes 4718608 | tf_op jit(solution)/shard_map/all_gather | solution.py:69
  153.8 5.6 %fusion = f32[96,384]{1,0:T(8,128)S(1)} fusion(f32[3072,384]{1,0:T(8,128)} %all-gather.5.cloned.1.call-done, f32[192,3072]{1,0:T(8,128)} %all-gather.3.cloned.1.call-done), kind=kOutput, calls=%fused_computation.1 | convolution fusion | flops 1358954496 | bytes 6045696 | tf_op jit(solution)/shard_map/dot_general | solution.py:54
  159.4 0.0 copy-done
  159.4 3.9 fusion.4
  163.3 2.5 copy.9
  165.9 0.0 reduce-scatter.3.cloned.1.call-update
  165.9 0.0 copy-start.1
  165.9 0.0 copy-start.2
  165.9 0.0 reduce-scatter.5.cloned.1.call-start
  166.0 17.3 %reduce-scatter.3.cloned.1.call-done = f32[16,96,384]{2,1,0:T(8,128)} async-done(((f32[32,96,384]{2,1,0:T(8,128)}), f32[16,96,384]{2,1,0:T(8,128)}) %reduce-scatter.3.cloned.1.call-update) | async-done | bytes 2359312 | tf_op jit(solution)/shard_map/reduce_scatter | solution.py:43
  183.3 0.0 reduce-scatter.5.cloned.1.call-update
  183.3 85.1 %reduce-scatter.5.cloned.1.call-done = f32[1,96,384]{2,1,0:T(8,128)} async-done(((f32[16,96,384]{2,1,0:T(8,128)}), f32[1,96,384]{2,1,0:T(8,128)}) %reduce-scatter.5.cloned.1.call-update) | async-done | bytes 147472 | tf_op jit(solution)/shard_map/reduce_scatter | solution.py:44
  268.4 0.0 copy-done.1
  268.4 0.0 copy-done.2
  268.4 1.7 add_divide_fusion
  270.1 0.0 slice-start
  270.1 0.5 stack.2
  270.6 0.0 slice-start.1
  270.7 116.1 %all_to_all.10 = f32[32,96,384]{2,1,0:T(8,128)S(1)} all-to-all(f32[32,96,384]{2,1,0:T(8,128)S(1)} %stack.2), channel_id=1, replica_groups=mesh['wide_0'=4,'wide_1'=4,'wide_2'=2,'narrow'=8] {'wide_0','wide_1','wi..., dimensions={0} | all-to-all | bytes 9437184 | tf_op jit(solution)/shard_map/all_to_all | solution.py:16
  386.7 2.9 fusion.2
  389.7 0.0 slice-done
  389.7 0.0 slice-done.1
  389.7 4.6 %fusion.10 = f32[96,3072]{1,0:T(8,128)S(1)} fusion(f32[96,384]{1,0:T(8,128)S(1)} %fusion.2, f32[3072,384]{1,0:T(8,128)S(1)} %bitcast.25), kind=kOutput, calls=%fused_computation.13 | convolution fusion | flops 1358954496 | bytes 6045696 | tf_op jit(solution)/shard_map/dot_general | solution.py:58
  394.3 0.1 copy.13
  394.4 42.3 %all_to_all.11 = f32[8,96,384]{2,1,0:T(8,128)S(1)} all-to-all(f32[8,96,384]{2,1,0:T(8,128)S(1)} %bitcast.29), channel_id=1, replica_groups=mesh['wide_0'=4,'wide_1'=4,'wide_2'=2,'narrow'=8] {'narrow'}, dimensions={0} | all-to-all | bytes 2359296 | tf_op jit(solution)/shard_map/all_to_all | solution.py:49
  436.7 0.7 reduce_sum.9
  (1 shorter events, 0.0 us)
Async XLA Ops:
  7.2 84.6 %all-gather.3.cloned.1.call-start = ((), (), s32[]{:S(2)}) async-start(), calls=%async_computation.4 | async-start | bytes 2654208 | tf_op jit(solution)/shard_map/all_gather | solution.py:29
  8.9 144.8 %all-gather.5.cloned.1.call-start = ((), (), s32[]{:S(2)}) async-start(), calls=%async_computation.5 | async-start | bytes 4866048 | tf_op jit(solution)/shard_map/all_gather | solution.py:69
  9.7 173.6 %reduce-scatter.3.cloned.1.call-start = ((), (), s32[]{:S(2)}) async-start(), calls=%async_computation.6 | async-start | bytes 7077888 | tf_op jit(solution)/shard_map/reduce_scatter | solution.py:43
  91.8 67.6 %copy-start = (f32[192,3072]{1,0:T(8,128)S(1)}, f32[192,3072]{1,0:T(8,128)}, u32[]{:S(2)}) copy-start(f32[192,3072]{1,0:T(8,128)} %all-gather.3.cloned.1.call-done) | copy-start | bytes 7077892
  165.9 102.5 %copy-start.1 = (f32[96,384]{1,0:T(8,128)S(1)}, f32[96,384]{1,0:T(8,128)}, u32[]{:S(2)}) copy-start(f32[96,384]{1,0:T(8,128)} %param.6) | copy-start | bytes 442372
  165.9 102.5 %copy-start.2 = (f32[96,384]{1,0:T(8,128)S(1)}, f32[96,384]{1,0:T(8,128)}, u32[]{:S(2)}) copy-start(f32[96,384]{1,0:T(8,128)} %param.7) | copy-start | bytes 442372
  165.9 102.5 %reduce-scatter.5.cloned.1.call-start = ((), (), s32[]{:S(2)}) async-start(), calls=%async_computation.7 | async-start | bytes 2506752 | tf_op jit(solution)/shard_map/reduce_scatter | solution.py:44
  270.1 119.6 %slice-start = ((s8[4718592]{0:T(1024)(128)(4,1)}), s8[4194304]{0:T(1024)(128)(4,1)S(1)}, s32[]{:S(2)}) async-start(s8[4718592]{0:T(1024)(128)(4,1)} %bitcast.24), calls=%async_computation.8 | async-start | bytes 8388608
  270.6 119.0 %slice-start.1 = ((s8[4718592]{0:T(1024)(128)(4,1)}), s8[524288]{0:T(1024)(128)(4,1)S(1)}, s32[]{:S(2)}) async-start(s8[4718592]{0:T(1024)(128)(4,1)} %bitcast.24), calls=%async_computation.9 | async-start | bytes 1048576
Sparse Core Ops, SparseCore 0:
  10.6 81.1 all-gather.2
  93.7 60.0 all-gather.4
  166.0 17.2 reduce-scatter.2
  185.8 82.5 reduce-scatter.4
